TPU v7x, 32 devices: a whole 2x2x4 slice. The times are simulated.
32 devices in a mesh: ctx: 4 (over z), exp: 8 (over y, x, core).
Axes of the slice: x: 2, y: 2, z: 4, core: 2. Of those that a mesh axis runs over, the one named last changes fastest.
Arguments:
- out_grad: bfloat16 [4096, 2048], P(('ctx', 'exp')), may hold values from -6 to 6
- route_ids: int32 [4096, 4], P(('ctx', 'exp')), may hold values from 0 to 15, all different within a row; in each aligned block of 128 rows (0 to 127, 128 to 255, ...) at most 36 rows name the same one
- gate_probs: float32 [4096, 4], P(('ctx', 'exp')), may hold values from 0 to 1, as said below
- saved_hidden: bfloat16 [4, 8, 16, 36, 768], P('ctx', None, 'exp'), may hold values from -6 to 6
- down_weight: bfloat16 [16, 768, 2048], P('exp', None, 'ctx'), may hold values from -0.02734375 to 0.02734375
- router_weight: bfloat16 [2048, 16], replicated, may hold values from -1.5 to 1.5
- proj_weight: bfloat16 [4096, 2048], P('ctx'), may hold values from -0.125 to 0.125
Outputs:
- head_grads: bfloat16 [4, 1024, 4096], P(None, 'exp', 'ctx')
- router_grad: float32 [4096, 4], P(('ctx', 'exp'))
Inputs may be any that keep to these rules, and one draw needn't show every extreme that they name: `route_ids`: each token names 4 different experts; among the tokens of one device no expert is named more than 36 times, and in some device some expert is named exactly 36 times. `gate_probs`: positive; a token's 4 gates sum to one.
All inputs are finite; a program needn't handle non-finite values.
Results may differ from a plain program's by a relative error of at most 0.009.
Values may be sent and summed in bfloat16 or wider, within the bound.
A program may use at most 64 MiB of HBM per device.

v0:
```python
import jax
import jax.numpy as jnp
from jax import lax
from jax.sharding import PartitionSpec as P


def route_ranks(route_ids, experts):
    flat_ids = route_ids.reshape(-1)
    onehot = (flat_ids[:, None] == jnp.arange(experts, dtype=jnp.int32)[None, :]).astype(jnp.int32)
    earlier = jnp.cumsum(onehot, axis=0) - onehot
    slot_rank = jnp.sum(earlier * onehot, axis=1)
    return (flat_ids, slot_rank)


def shards(out_grad, route_ids, gate_probs, saved_hidden, down_weight, router_weight, proj_weight):
    tok_rows, top_count = route_ids.shape
    experts = router_weight.shape[1]
    groups = lax.axis_size("exp")
    local_experts = down_weight.shape[0]
    capacity = saved_hidden.shape[3]
    arrived_rows = lax.all_gather(out_grad, "ctx", axis=0, tiled=True)
    flat_ids, slot_rank = route_ranks(route_ids, experts)
    positions = flat_ids * capacity + slot_rank
    hidden_local = saved_hidden[0]
    spread = jnp.repeat(out_grad, top_count, axis=0)
    send_rows = (
        jnp.zeros((experts * capacity, out_grad.shape[1]), out_grad.dtype).at[positions].set(spread)
    )
    send_rows = send_rows.reshape(groups, local_experts, capacity, out_grad.shape[1])
    arrived = lax.all_to_all(send_rows, "exp", split_axis=0, concat_axis=0, tiled=True)
    outputs = jnp.einsum(
        "secf,efn->secn",
        hidden_local,
        lax.all_gather(down_weight, "ctx", axis=2, tiled=True),
        preferred_element_type=jnp.float32,
    ).astype(jnp.bfloat16)
    partial_grad = jnp.sum(arrived.astype(jnp.float32) * outputs.astype(jnp.float32), axis=3)
    returned = lax.all_to_all(partial_grad, "exp", split_axis=0, concat_axis=0, tiled=True)
    gate_grad = returned.reshape(-1)[positions].reshape(tok_rows, top_count)
    weighted = jnp.sum(gate_probs * gate_grad, axis=1, keepdims=True)
    router_grad = gate_probs * (gate_grad - weighted)
    matches = route_ids[:, :, None] == jnp.arange(experts, dtype=jnp.int32)[None, None, :]
    dense_grad = jnp.sum(jnp.where(matches, router_grad[:, :, None], 0.0), axis=1)
    router_wide = router_weight.astype(jnp.float32)
    dense_all = lax.all_gather(dense_grad.astype(jnp.bfloat16), "ctx", axis=0, tiled=True).astype(
        dense_grad.dtype
    )
    combined = (
        arrived_rows.astype(jnp.float32)
        + lax.dot_general(
            dense_all, router_wide, (((1,), (1,)), ((), ())), precision=lax.Precision.HIGHEST
        )
    ).astype(jnp.bfloat16)
    head_flat = lax.dot_general(
        combined, proj_weight, (((1,), (1,)), ((), ())), preferred_element_type=jnp.float32
    ).astype(jnp.bfloat16)
    head_grads = head_flat.reshape(lax.axis_size("ctx"), tok_rows, proj_weight.shape[0])
    return (head_grads, router_grad)


def solution(mesh):
    return jax.shard_map(
        shards,
        mesh=mesh,
        in_specs=(
            P(("ctx", "exp"), None),
            P(("ctx", "exp"), None),
            P(("ctx", "exp"), None),
            P("ctx", None, "exp", None, None),
            P("exp", None, "ctx"),
            P(),
            P("ctx", None),
        ),
        out_specs=(P(None, "exp", "ctx"), P(("ctx", "exp"), None)),
        check_vma=False,
    )
```

profile of v0, /device:TPU:0, one launch (start us, length us, event | category | flops | bytes accessed | tf_op | source)
XLA Modules:
  0.0 186.4 jit_solution(17179931395707088919)
XLA Ops:
  7.2 0.7 all-gather.5.cloned.1.call-update
  7.9 0.8 copy.58
  8.9 1.2 reduce-window.6
  10.1 0.2 slice_reduce_fusion
  10.4 0.7 broadcast_multiply_fusion
  11.3 1.0 broadcast_in_dim.26
  12.3 2.1 %reshape.86 = bf16[512,2048]{1,0:T(8,128)(2,1)} reshape(bf16[128,4,2048]{2,1,0:T(4,128)(2,1)S(1)} %broadcast_in_dim.26) | data formatting | bytes 4194304 | tf_op jit(solution)/shard_map/reshape | solution.py:25
  14.6 6.3 %scatter_custom_fusion = bf16[576,2048]{1,0:T(8,128)(2,1)} fusion(s32[512]{0:T(512)S(1)} %bitcast.41, bf16[512,2048]{1,0:T(8,128)(2,1)} %reshape.86, bf16[]{:T(256)} %constant.5.clone.1), kind=kCustom, calls=%fused_computation.9 | custom fusion | bytes 2359808 | tf_op jit(solution)/shard_map/scatter | solution.py:27
  20.9 2.7 %reshape.70 = bf16[8,2,36,2048]{3,2,1,0:T(8,128)(2,1)S(1)} reshape(bf16[576,2048]{1,0:T(8,128)(2,1)} %scatter_custom_fusion) | data formatting | bytes 4718592 | tf_op jit(solution)/shard_map/reshape | solution.py:29
  23.6 3.9 %copy.61 = bf16[8,2,36,2048]{3,1,2,0:T(2,128)(2,1)} copy(bf16[8,2,36,2048]{3,2,1,0:T(8,128)(2,1)S(1)} %reshape.70) | data formatting | bytes 4718592 | tf_op jit(solution)/shard_map/reshape | solution.py:29
  27.5 5.2 %all-to-all-start = ((bf16[8,2,36,2048]{3,1,2,0:T(2,128)(2,1)}), bf16[8,2,36,2048]{3,1,2,0:T(2,128)(2,1)S(1)}, u32[]{:S(2)}, u32[]{:S(2)}) async-start(bf16[8,2,36,2048]{3,1,2,0:T(2,128)(2,1)} %copy.61), calls=%async_computation | async-start | bytes 4718592 | tf_op jit(solution)/shard_map/all_to_all | solution.py:30
  32.7 0.7 all-gather.3.cloned.1.call-update
  33.4 28.7 %all-to-all-done = bf16[8,2,36,2048]{3,1,2,0:T(2,128)(2,1)S(1)} async-done(((bf16[8,2,36,2048]{3,1,2,0:T(2,128)(2,1)}), bf16[8,2,36,2048]{3,1,2,0:T(2,128)(2,1)S(1)}, u32[]{:S(2)}, u32[]{:S(2)}) %all-to-all-start) | async-done | bytes 2359328 | tf_op jit(solution)/shard_map/all_to_all | solution.py:30
  62.1 65.6 %all-gather.5.cloned.1.call-done = bf16[2,768,2048]{2,1,0:T(8,128)(2,1)} async-done(((bf16[2,768,512]{2,1,0:T(8,128)(2,1)}), bf16[2,768,2048]{2,1,0:T(8,128)(2,1)}) %all-gather.5.cloned.1.call-update) | async-done | bytes 6291472 | tf_op jit(solution)/shard_map/all_gather | solution.py:34
  127.7 6.1 %fusion.2 = f32[8,2,36]{2,0,1:T(8,128)S(1)} fusion(bf16[8,2,36,2048]{3,1,2,0:T(2,128)(2,1)S(1)} %all-to-all-done, bf16[2,768,2048]{2,1,0:T(8,128)(2,1)} %all-gather.5.cloned.1.call-done, bf16[8,2,36,768]{3,1,2,0:T(2,128)(2,1)S(1)} %bitcast.40), kind=kOutput, calls=%fused_computation.5 | convolution fusion | flops 1817837056 | bytes 9537792 | tf_op jit(solution)/shard_map/secf,efn->secn/dot_general | solution.py:31
  133.8 0.6 copy.64
  134.4 3.8 %all-to-all-start.1 = ((f32[8,2,36]{2,1,0:T(2,128)}), f32[8,2,36]{2,1,0:T(2,128)S(1)}, u32[]{:S(2)}, u32[]{:S(2)}) async-start(f32[8,2,36]{2,1,0:T(2,128)} %copy.64), calls=%async_computation.1 | async-start | bytes 16384 | tf_op jit(solution)/shard_map/all_to_all | solution.py:38
  138.4 4.6 %all-to-all-done.1 = f32[8,2,36]{2,1,0:T(2,128)S(1)} async-done(((f32[8,2,36]{2,1,0:T(2,128)}), f32[8,2,36]{2,1,0:T(2,128)S(1)}, u32[]{:S(2)}, u32[]{:S(2)}) %all-to-all-start.1) | async-done | bytes 2336 | tf_op jit(solution)/shard_map/all_to_all | solution.py:38
  143.1 2.3 %gather_fusion = f32[512]{0:T(512)S(1)} fusion(f32[576]{0:T(1024)S(1)} %reshape.71, s32[1024]{0:T(1024)S(1)} %pad_clamp_fusion), kind=kCustom, calls=%fused_computation | custom fusion | bytes 6144 | tf_op jit(solution)/shard_map/gather | solution.py:39
  145.8 12.6 %all_gather.11 = bf16[512,16]{0,1:T(8,128)(2,1)S(1)} all-gather(bf16[128,16]{0,1:T(8,128)(2,1)S(1)} %select_reduce_fusion), channel_id=1, replica_groups=mesh['ctx'=4,'exp'=8] {'ctx'}, dimensions={0}, use_global_device_ids=true | all-gather | bytes 20480 | tf_op jit(solution)/shard_map/all_gather | solution.py:45
  158.4 15.0 %all-gather.3.cloned.1.call-done = bf16[512,2048]{1,0:T(8,128)(2,1)} async-done(((bf16[128,2048]{1,0:T(8,128)(2,1)}), bf16[512,2048]{1,0:T(8,128)(2,1)}) %all-gather.3.cloned.1.call-update) | async-done | bytes 2097168 | tf_op jit(solution)/shard_map/all_gather | solution.py:21
  173.4 2.5 %add_convert_fusion = bf16[512,2048]{1,0:T(8,128)(2,1)S(1)} fusion(bf16[512,2048]{1,0:T(8,128)(2,1)} %all-gather.3.cloned.1.call-done, bf16[512,16]{0,1:T(8,128)(2,1)S(1)} %all_gather.11, bf16[2048,16]{0,1:T(8,128)(2,1)S(1)} %copy-done.2), kind=kOutput, calls=%fused_computation.6 | convolution fusion | flops 36700160 | bytes 4276224 | tf_op jit(solution)/shard_map/dot_general | solution.py:50
  175.8 0.3 copy-done.6
  176.2 3.3 %convolution_convert_fusion = bf16[512,1024]{1,0:T(8,128)(2,1)} fusion(bf16[512,2048]{1,0:T(8,128)(2,1)S(1)} %add_convert_fusion, bf16[1024,2048]{1,0:T(8,128)(2,1)S(1)} %copy-done.6), kind=kOutput, calls=%fused_computation.8 | convolution fusion | flops 2148007936 | bytes 7340032 | tf_op jit(solution)/shard_map/dot_general | solution.py:54
  (32 shorter events, 1.3 us)
Async XLA Ops:
  7.2 120.5 %copy-start = (bf16[1,8,2,36,768]{4,2,3,1,0:T(2,128)(2,1)S(1)}, bf16[1,8,2,36,768]{4,2,3,1,0:T(2,128)(2,1)}, u32[]{:S(2)}) copy-start(bf16[1,8,2,36,768]{4,2,3,1,0:T(2,128)(2,1)} %param.10) | copy-start | bytes 2654212
  7.2 4.1 %copy-start.1 = (bf16[128,2048]{1,0:T(8,128)(2,1)S(1)}, bf16[128,2048]{1,0:T(8,128)(2,1)}, u32[]{:S(2)}) copy-start(bf16[128,2048]{1,0:T(8,128)(2,1)} %param.7) | copy-start | bytes 1572868
  7.2 120.5 %all-gather.5.cloned.1.call-start = ((), (), s32[]{:S(2)}) async-start(), calls=%async_computation.3 | async-start | bytes 7864320 | tf_op jit(solution)/shard_map/all_gather | solution.py:34
  27.5 34.6 %all-to-all-start = ((bf16[8,2,36,2048]{3,1,2,0:T(2,128)(2,1)}), bf16[8,2,36,2048]{3,1,2,0:T(2,128)(2,1)S(1)}, u32[]{:S(2)}, u32[]{:S(2)}) async-start(bf16[8,2,36,2048]{3,1,2,0:T(2,128)(2,1)} %copy.61), calls=%async_computation | async-start | bytes 4718592 | tf_op jit(solution)/shard_map/all_to_all | solution.py:30
  32.7 140.7 %all-gather.3.cloned.1.call-start = ((), (), s32[]{:S(2)}) async-start(), calls=%async_computation.2 | async-start | bytes 2621440 | tf_op jit(solution)/shard_map/all_gather | solution.py:21
  127.7 10.6 %copy-start.5 = (f32[128,4]{0,1:T(4,128)S(1)}, f32[128,4]{0,1:T(4,128)}, u32[]{:S(2)}) copy-start(f32[128,4]{0,1:T(4,128)} %param.9) | copy-start | bytes 6148
  133.8 11.9 %copy-start.3 = (s32[128,4]{0,1:T(4,128)S(1)}, s32[128,4]{0,1:T(4,128)}, u32[]{:S(2)}) copy-start(s32[128,4]{0,1:T(4,128)} %param.8) | copy-start | bytes 6148
  133.8 39.6 %copy-start.2 = (bf16[2048,16]{0,1:T(8,128)(2,1)S(1)}, bf16[2048,16]{0,1:T(8,128)(2,1)}, u32[]{:S(2)}) copy-start(bf16[2048,16]{0,1:T(8,128)(2,1)} %param.12) | copy-start | bytes 196612
  134.4 8.5 %all-to-all-start.1 = ((f32[8,2,36]{2,1,0:T(2,128)}), f32[8,2,36]{2,1,0:T(2,128)S(1)}, u32[]{:S(2)}, u32[]{:S(2)}) async-start(f32[8,2,36]{2,1,0:T(2,128)} %copy.64), calls=%async_computation.1 | async-start | bytes 16384 | tf_op jit(solution)/shard_map/all_to_all | solution.py:38
  145.7 33.8 %copy-start.4 = (f32[128,4]{0,1:T(4,128)}, f32[128,4]{0,1:T(4,128)S(1)}, u32[]{:S(2)}) copy-start(f32[128,4]{0,1:T(4,128)S(1)} %copy.67) | copy-start | bytes 6148
  173.4 2.8 %copy-start.6 = (bf16[1024,2048]{1,0:T(8,128)(2,1)S(1)}, bf16[1024,2048]{1,0:T(8,128)(2,1)}, u32[]{:S(2)}) copy-start(bf16[1024,2048]{1,0:T(8,128)(2,1)} %param.13) | copy-start | bytes 12582916
Sparse Core Ops, SparseCore 0:
  9.6 118.0 all-gather.4
  129.2 44.0 all-gather.2
where the time goes:
time: 187 us; the launch traced here: 186 us
  waiting for transfers between devices  115 us (61%)
  local copies, waits for them, and re-layouts  21.1 us (11%)
  between operations  14.2 us (8%)
  blocking collectives  12.6 us (7%)
  matrix products  11.9 us (6%)
  starting transfers between devices  9.12 us (5%)
  other arithmetic  2.22 us (1%)
    all_gather x1, waiting for transfers between devices, shards(): lax.all_gather(down_weight, 'ctx', axis=2, tiled=True)  65.6 us
    all_to_all x1, waiting for transfers between devices, shards(): lax.all_to_all(send_rows, 'exp', split_axis=0, concat_axis=0, tiled=True)  28.7 us
    all_gather x1, waiting for transfers between devices, shards(): arrived_rows = lax.all_gather(out_grad, 'ctx', axis=0, tiled=True)  15 us
    all_gather x1, blocking collectives, shards(): lax.all_gather(dense_grad.astype(jnp.bfloat16), 'ctx', axis=0, tiled=True)  12.6 us
    reshape x2, local copies, waits for them, and re-layouts, shards(): send_rows.reshape(groups, local_experts, capacity, out_grad.shape[1])  6.6 us
    scatter x1, local copies, waits for them, and re-layouts, shards(): jnp.zeros((experts * capacity, out_grad.shape[1]), out_grad.dtype)  6.29 us
    dot_general x1, matrix products, shards(): jnp.einsum('secf,efn->secn', hidden_local, lax.all_gather(down_weight, 'c...  6.13 us
    all_to_all x1, starting transfers between devices, shards(): lax.all_to_all(send_rows, 'exp', split_axis=0, concat_axis=0, tiled=True)  5.21 us
  transfers between devices with their start and end apart: 4, of which 4 were waited for; matrix products, arithmetic and copies ran while one was open for 16% of the time, Pallas kernels for 0%

commit v1 on v0

v1 whole, which is shorter than its diff:
```python
import jax
import jax.numpy as jnp
from jax import lax
from jax.sharding import PartitionSpec as P


def route_ranks(route_ids, experts):
    flat_ids = route_ids.reshape(-1)
    onehot = (flat_ids[:, None] == jnp.arange(experts, dtype=jnp.int32)[None, :]).astype(jnp.int32)
    earlier = jnp.cumsum(onehot, axis=0) - onehot
    slot_rank = jnp.sum(earlier * onehot, axis=1)
    return (flat_ids, slot_rank)


def shards(out_grad, route_ids, gate_probs, saved_hidden, down_weight, router_weight, proj_weight):
    tok_rows, top_count = route_ids.shape
    experts = router_weight.shape[1]
    groups = lax.axis_size("exp")
    n_ctx = lax.axis_size("ctx")
    local_experts = down_weight.shape[0]
    capacity = saved_hidden.shape[3]
    dslice = down_weight.shape[2]
    me_ctx = lax.axis_index("ctx")
    rows_all = lax.all_gather(out_grad, "ctx", axis=0, tiled=False)
    ids_all = lax.all_gather(route_ids, "ctx", axis=0, tiled=False)
    probs_all = lax.all_gather(gate_probs, "ctx", axis=0, tiled=False)
    hidden_all = lax.all_gather(saved_hidden[0], "ctx", axis=0, tiled=False)
    flat_ids, slot_rank = jax.vmap(lambda r: route_ranks(r, experts))(ids_all)
    positions = flat_ids * capacity + slot_rank
    cols = lax.dynamic_slice_in_dim(rows_all, me_ctx * dslice, dslice, axis=2)
    spread = jnp.repeat(cols, top_count, axis=1)
    blk = jnp.broadcast_to(jnp.arange(n_ctx, dtype=jnp.int32)[:, None], flat_ids.shape)
    send_rows = jnp.zeros(
        (groups, n_ctx, local_experts, capacity, dslice), out_grad.dtype
    ).at[flat_ids // local_experts, blk, flat_ids % local_experts, slot_rank].set(spread)
    arrived = lax.all_to_all(send_rows, "exp", split_axis=0, concat_axis=0, tiled=True)
    outputs = jnp.einsum(
        "csekf,efn->scekn", hidden_all, down_weight, preferred_element_type=jnp.float32
    ).astype(jnp.bfloat16)
    partial_grad = jnp.sum(arrived.astype(jnp.float32) * outputs.astype(jnp.float32), axis=4)
    returned = lax.all_to_all(partial_grad, "exp", split_axis=0, concat_axis=0, tiled=True)
    returned = lax.psum(returned, "ctx")
    returned = jnp.transpose(returned, (1, 0, 2, 3)).reshape(n_ctx, experts * capacity)
    gate_grad = jnp.take_along_axis(returned, positions, axis=1).reshape(n_ctx, tok_rows, top_count)
    weighted = jnp.sum(probs_all * gate_grad, axis=2, keepdims=True)
    router_all = probs_all * (gate_grad - weighted)
    matches = ids_all[:, :, :, None] == jnp.arange(experts, dtype=jnp.int32)[None, None, None, :]
    dense_all = jnp.sum(jnp.where(matches, router_all[:, :, :, None], 0.0), axis=2)
    router_wide = router_weight.astype(jnp.float32)
    combined = (
        rows_all.astype(jnp.float32)
        + lax.dot_general(
            dense_all, router_wide, (((2,), (1,)), ((), ())), precision=lax.Precision.HIGHEST
        )
    ).astype(jnp.bfloat16)
    head_flat = lax.dot_general(
        combined.reshape(n_ctx * tok_rows, -1),
        proj_weight,
        (((1,), (1,)), ((), ())),
        preferred_element_type=jnp.float32,
    ).astype(jnp.bfloat16)
    head_grads = head_flat.reshape(n_ctx, tok_rows, proj_weight.shape[0])
    router_grad = lax.dynamic_index_in_dim(router_all, me_ctx, axis=0, keepdims=False)
    return (head_grads, router_grad)


def solution(mesh):
    return jax.shard_map(
        shards,
        mesh=mesh,
        in_specs=(
            P(("ctx", "exp"), None),
            P(("ctx", "exp"), None),
            P(("ctx", "exp"), None),
            P("ctx", None, "exp", None, None),
            P("exp", None, "ctx"),
            P(),
            P("ctx", None),
        ),
        out_specs=(P(None, "exp", "ctx"), P(("ctx", "exp"), None)),
        check_vma=False,
    )
```

time: 187 us -> 209 us (1.12)
  waiting for transfers between devices: 115 us -> 45.7 us
  blocking collectives: 12.6 us -> 74.2 us
  local copies, waits for them, and re-layouts: 21.1 us -> 51.6 us
  starting transfers between devices: 9.12 us -> 3.73 us
  other arithmetic: 2.22 us -> 5.97 us
    all_gather x2, waiting for transfers between devices: 80.5 us -> 45 us  [the longest x1 28 us: shards(): rows_all = lax.all_gather(out_grad, 'ctx', axis=0, tiled=False)]
    all_to_all x0 -> x1, blocking collectives: none -> 32.9 us  [shards(): lax.all_to_all(send_rows, 'exp', split_axis=0, concat_axis=0, tiled=True)]
    all_to_all x1 -> x0, waiting for transfers between devices: 28.7 us -> none  [shards(): lax.all_to_all(send_rows, 'exp', split_axis=0, concat_axis=0, tiled=True)]
    unnamed x16 -> x21, local copies, waits for them, and re-layouts: 1.28 us -> 20.7 us
    psum x0 -> x1, blocking collectives: none -> 15.7 us  [shards(): returned = lax.psum(returned, 'ctx')]
    gather x1 -> x2, local copies, waits for them, and re-layouts: 2.29 us -> 18 us  [shards(): jnp.take_along_axis(returned, positions, axis=1)]
    all_gather x1 -> x2, blocking collectives: 12.6 us -> 25.6 us  [the longest x1 13.6 us: shards(): ids_all = lax.all_gather(route_ids, 'ctx', axis=0, tiled=False)]
    all_to_all x1 -> x0, starting transfers between devices: 5.21 us -> none  [shards(): lax.all_to_all(send_rows, 'exp', split_axis=0, concat_axis=0, tiled=True)]
  transfers between devices with their start and end apart: 4 -> 3, of which waited for: 4 -> 2; matrix products, arithmetic and copies ran while one was open for 16% -> 17% of each run, Pallas kernels for 0% -> 0%
where the time goes in v1:
time: 209 us; the launch traced here: 208 us
  blocking collectives  74.2 us (36%)
  local copies, waits for them, and re-layouts  51.6 us (25%)
  waiting for transfers between devices  45.7 us (22%)
  between operations  14.3 us (7%)
  matrix products  12.5 us (6%)
  other arithmetic  5.97 us (3%)
  starting transfers between devices  3.73 us (2%)
    all_to_all x1, blocking collectives, shards(): lax.all_to_all(send_rows, 'exp', split_axis=0, concat_axis=0, tiled=True)  32.9 us
    all_gather x1, waiting for transfers between devices, shards(): rows_all = lax.all_gather(out_grad, 'ctx', axis=0, tiled=False)  28 us
    unnamed x21, local copies, waits for them, and re-layouts  20.7 us
    gather x2, local copies, waits for them, and re-layouts, shards(): jnp.take_along_axis(returned, positions, axis=1)  18 us
    all_gather x1, waiting for transfers between devices, shards(): hidden_all = lax.all_gather(saved_hidden[0], 'ctx', axis=0, tiled=False)  17 us
    psum x1, blocking collectives, shards(): returned = lax.psum(returned, 'ctx')  15.7 us
    all_gather x1, blocking collectives, shards(): ids_all = lax.all_gather(route_ids, 'ctx', axis=0, tiled=False)  13.6 us
    all_gather x1, blocking collectives, shards(): probs_all = lax.all_gather(gate_probs, 'ctx', axis=0, tiled=False)  11.9 us
  transfers between devices with their start and end apart: 3, of which 2 were waited for; matrix products, arithmetic and copies ran while one was open for 17% of the time, Pallas kernels for 0%

profile of v1, /device:TPU:0, one launch (start us, length us, event | category | flops | bytes accessed | tf_op | source)
XLA Modules:
  0.0 208.0 jit_solution(2434617461053370310)
XLA Ops:
  7.2 0.7 all-gather.8.cloned.1.call-update
  8.0 2.2 %copy.53 = bf16[1,8,2,36,768]{4,3,1,0,2:T(8,128)(2,1)} copy(bf16[1,8,2,36,768]{4,2,3,1,0:T(2,128)(2,1)} %param.10) | data formatting | bytes 1769472 | tf_op args[3]
  10.2 13.6 %all-gather.1 = s32[512,4]{0,1:T(4,128)S(1)} all-gather(s32[128,4]{0,1:T(4,128)S(1)} %copy-done.2), channel_id=3, replica_groups=mesh['ctx'=4,'exp'=8] {'ctx'}, dimensions={0}, use_global_device_ids=true | all-gather | bytes 10240 | tf_op jit(solution)/shard_map/all_gather | solution.py:25
  24.6 4.6 %reduce-window.6 = s32[4,16,4,128]{3,1,2,0:T(8,128)S(1)} reduce-window(s32[4,16,4,128]{3,1,2,0:T(8,128)S(1)} %fusion.7, s32[]{:T(128)} %constant.58.clone.1), window={size=1x1x1x128 pad=0_0x0_0x0_0x127_0}, to_apply=%region_0.0 | reduce-window | flops 4161536 | bytes 262148 | tf_op jit(solution)/shard_map/reduce-window
  30.0 28.0 %all-gather.8.cloned.1.call-done = bf16[512,2048]{1,0:T(8,128)(2,1)} async-done(((bf16[128,2048]{1,0:T(8,128)(2,1)}), bf16[512,2048]{1,0:T(8,128)(2,1)}) %all-gather.8.cloned.1.call-update) | async-done | bytes 2097168 | tf_op jit(solution)/shard_map/all_gather | solution.py:24
  58.0 1.1 constant_dynamic-slice_fusion.1
  59.1 1.9 broadcast_in_dim.20
  61.0 4.0 %reshape.236 = bf16[2048,512]{1,0:T(8,128)(2,1)} reshape(bf16[4,128,4,512]{3,2,1,0:T(4,128)(2,1)} %broadcast_in_dim.20) | data formatting | bytes 4194304 | tf_op jit(solution)/shard_map/reshape | solution.py:31
  65.0 11.7 %scatter_custom_fusion = bf16[2304,512]{1,0:T(8,128)(2,1)} fusion(s32[2048]{0:T(1024)S(1)} %bitcast.66, bf16[2048,512]{1,0:T(8,128)(2,1)} %reshape.236, bf16[]{:T(256)} %constant.61.clone.1), kind=kCustom, calls=%fused_computation.7 | custom fusion | bytes 2359808
  76.7 5.9 %reshape.226 = bf16[8,4,36,2,512]{4,3,2,1,0:T(2,128)(2,1)} reshape(bf16[2304,512]{1,0:T(8,128)(2,1)} %scatter_custom_fusion) | data formatting | bytes 4718592
  82.6 2.9 %copy.51 = bf16[8,4,2,36,512]{4,1,3,2,0:T(4,128)(2,1)S(1)} copy(bf16[8,4,2,36,512]{4,2,3,1,0:T(2,128)(2,1)} %bitcast.60) | data formatting | bytes 4718592 | tf_op jit(solution)/shard_map/scatter | solution.py:35
  85.5 32.9 %all_to_all.10 = bf16[8,4,2,36,512]{4,1,3,2,0:T(4,128)(2,1)} all-to-all(bf16[8,4,2,36,512]{4,1,3,2,0:T(4,128)(2,1)S(1)} %copy.51), channel_id=1, replica_groups=mesh['ctx'=4,'exp'=8] {'exp'}, dimensions={0} | all-to-all | bytes 4718592 | tf_op jit(solution)/shard_map/all_to_all | solution.py:36
  118.4 17.0 %all-gather.6.cloned.1.call-done = bf16[4,8,2,36,768]{4,3,1,0,2:T(8,128)(2,1)} async-done(((bf16[1,8,2,36,768]{4,3,1,0,2:T(8,128)(2,1)}), bf16[4,8,2,36,768]{4,3,1,0,2:T(8,128)(2,1)}) %all-gather.6.cloned.1.call-update) | async-done | bytes 3538960 | tf_op jit(solution)/shard_map/all_gather | solution.py:27
  135.4 5.5 %fusion = f32[8,4,2,36]{3,0,1,2:T(8,128)S(1)} fusion(bf16[8,4,2,36,512]{4,1,3,2,0:T(4,128)(2,1)} %all_to_all.10, bf16[4,8,2,36,768]{4,3,1,0,2:T(8,128)(2,1)} %all-gather.6.cloned.1.call-done, bf16[2,768,512]{2,1,0:T(8,128)(2,1)S(1)} %copy-done), kind=kOutput, calls=%fused_computation.3 | convolution fusion | flops 1817835264 | bytes 7480320 | tf_op jit(solution)/shard_map/csekf,efn->scekn/dot_general | solution.py:37
  140.9 0.7 reshape.253
  141.6 3.7 %all-to-all-start.1 = ((f32[8,1,288]{2,1,0:T(1,128)}), f32[8,1,288]{2,1,0:T(1,128)S(1)}, u32[]{:S(2)}, u32[]{:S(2)}) async-start(f32[8,1,288]{2,1,0:T(1,128)} %reshape.253), calls=%async_computation.1 | async-start | bytes 24576 | tf_op jit(solution)/shard_map/all_to_all | solution.py:41
  145.6 11.9 %all-gather.2 = f32[512,4]{0,1:T(4,128)S(1)} all-gather(f32[128,4]{0,1:T(4,128)S(1)} %copy-done.3), channel_id=4, replica_groups=mesh['ctx'=4,'exp'=8] {'ctx'}, dimensions={0}, use_global_device_ids=true | all-gather | bytes 10240 | tf_op jit(solution)/shard_map/all_gather | solution.py:26
  157.8 0.5 broadcast.262
  158.3 0.7 reduce.6
  159.2 15.7 %psum.7 = f32[4,576]{1,0:T(4,128)S(1)} all-reduce(f32[4,576]{1,0:T(4,128)S(1)} %reshape.221), channel_id=1, replica_groups=mesh['ctx'=4,'exp'=8] {'ctx'}, use_global_device_ids=true, to_apply=%region_5.6 | all-reduce | flops 2304 | bytes 18432 | tf_op jit(solution)/shard_map/psum | solution.py:42
  174.9 17.7 %gather_fusion = f32[2048]{0:T(1024)S(1)} fusion(f32[4,576]{1,0:T(4,128)S(1)} %psum.7, s32[2048]{0:T(1024)S(1)} %bitcast.57), kind=kCustom, calls=%fused_computation | custom fusion | bytes 32768 | tf_op jit(solution)/shard_map/jit(take_along_axis)/gather | solution.py:44
  193.4 0.7 copy.57
  194.1 3.7 %add_convert_fusion = bf16[4,128,2048]{2,1,0:T(8,128)(2,1)S(1)} fusion(bf16[4,128,2048]{2,1,0:T(8,128)(2,1)} %bitcast.62, f32[4,128,16]{1,2,0:T(8,128)S(1)} %select_reduce_fusion, bf16[2048,16]{0,1:T(8,128)(2,1)S(1)} %copy-done.1), kind=kOutput, calls=%fused_computation.4 | convolution fusion | flops 204472320 | bytes 4292608 | tf_op jit(solution)/shard_map/dot_general | solution.py:52
  197.8 3.3 %convolution_convert_fusion = bf16[512,1024]{1,0:T(8,128)(2,1)} fusion(bf16[512,2048]{1,0:T(8,128)(2,1)S(1)} %bitcast.64, bf16[1024,2048]{1,0:T(8,128)(2,1)S(1)} %copy-done.6), kind=kOutput, calls=%fused_computation.6 | convolution fusion | flops 2148007936 | bytes 7340032 | tf_op jit(solution)/shard_map/dot_general | solution.py:56
  (47 shorter events, 3.1 us)
Async XLA Ops:
  7.2 128.2 %copy-start = (bf16[2,768,512]{2,1,0:T(8,128)(2,1)S(1)}, bf16[2,768,512]{2,1,0:T(8,128)(2,1)}, u32[]{:S(2)}) copy-start(bf16[2,768,512]{2,1,0:T(8,128)(2,1)} %param.11) | copy-start | bytes 4718596
  7.2 3.1 %copy-start.2 = (s32[128,4]{0,1:T(4,128)S(1)}, s32[128,4]{0,1:T(4,128)}, u32[]{:S(2)}) copy-start(s32[128,4]{0,1:T(4,128)} %param.8) | copy-start | bytes 6148
  7.2 50.8 %all-gather.8.cloned.1.call-start = ((), (), s32[]{:S(2)}) async-start(), calls=%async_computation.3 | async-start | bytes 2621440 | tf_op jit(solution)/shard_map/all_gather | solution.py:24
  7.9 21.9 %copy-start.5 = (s32[4]{0:T(128)S(1)}, s32[4]{0:T(128)}, u32[]{:S(2)}) copy-start(s32[4]{0:T(128)} %constant.74) | copy-start | bytes 52
  7.9 22.0 %copy-start.4 = (s32[4]{0:T(128)S(1)}, s32[4]{0:T(128)}, u32[]{:S(2)}) copy-start(s32[4]{0:T(128)} %constant.77) | copy-start | bytes 52
  7.9 127.4 %all-gather.6.cloned.1.call-start = ((), (), s32[]{:S(2)}) async-start(), calls=%async_computation.2 | async-start | bytes 4915200 | tf_op jit(solution)/shard_map/all_gather | solution.py:27
  118.4 27.2 %copy-start.3 = (f32[128,4]{0,1:T(4,128)S(1)}, f32[128,4]{0,1:T(4,128)}, u32[]{:S(2)}) copy-start(f32[128,4]{0,1:T(4,128)} %param.9) | copy-start | bytes 6148
  141.6 16.1 %all-to-all-start.1 = ((f32[8,1,288]{2,1,0:T(1,128)}), f32[8,1,288]{2,1,0:T(1,128)S(1)}, u32[]{:S(2)}, u32[]{:S(2)}) async-start(f32[8,1,288]{2,1,0:T(1,128)} %reshape.253), calls=%async_computation.1 | async-start | bytes 24576 | tf_op jit(solution)/shard_map/all_to_all | solution.py:41
  192.7 1.4 copy-start.1
  194.1 3.7 %copy-start.6 = (bf16[1024,2048]{1,0:T(8,128)(2,1)S(1)}, bf16[1024,2048]{1,0:T(8,128)(2,1)}, u32[]{:S(2)}) copy-start(bf16[1024,2048]{1,0:T(8,128)(2,1)} %param.13) | copy-start | bytes 12582916
Sparse Core Ops, SparseCore 0:
  9.6 48.4 all-gather.7
  60.2 75.1 all-gather.5

commit v2 on v1

--- a/solution.py
+++ b/solution.py
@@ -22,8 +22,10 @@
     dslice = down_weight.shape[2]
     me_ctx = lax.axis_index("ctx")
     rows_all = lax.all_gather(out_grad, "ctx", axis=0, tiled=False)
-    ids_all = lax.all_gather(route_ids, "ctx", axis=0, tiled=False)
-    probs_all = lax.all_gather(gate_probs, "ctx", axis=0, tiled=False)
+    packed = jnp.concatenate([route_ids.astype(jnp.float32), gate_probs], axis=1)
+    packed_all = lax.all_gather(packed, "ctx", axis=0, tiled=False)
+    ids_all = packed_all[:, :, :top_count].astype(jnp.int32)
+    probs_all = packed_all[:, :, top_count:]
     hidden_all = lax.all_gather(saved_hidden[0], "ctx", axis=0, tiled=False)
     flat_ids, slot_rank = jax.vmap(lambda r: route_ranks(r, experts))(ids_all)
     positions = flat_ids * capacity + slot_rank
@@ -41,7 +43,9 @@
     returned = lax.all_to_all(partial_grad, "exp", split_axis=0, concat_axis=0, tiled=True)
     returned = lax.psum(returned, "ctx")
     returned = jnp.transpose(returned, (1, 0, 2, 3)).reshape(n_ctx, experts * capacity)
-    gate_grad = jnp.take_along_axis(returned, positions, axis=1).reshape(n_ctx, tok_rows, top_count)
+    picks = positions[:, :, None] == jnp.arange(experts * capacity, dtype=jnp.int32)[None, None, :]
+    gate_grad = jnp.sum(jnp.where(picks, returned[:, None, :], 0.0), axis=2)
+    gate_grad = gate_grad.reshape(n_ctx, tok_rows, top_count)
     weighted = jnp.sum(probs_all * gate_grad, axis=2, keepdims=True)
     router_all = probs_all * (gate_grad - weighted)
     matches = ids_all[:, :, :, None] == jnp.arange(experts, dtype=jnp.int32)[None, None, None, :]

time: 209 us -> 184 us (0.88)
  local copies, waits for them, and re-layouts: 51.6 us -> 33.4 us
  blocking collectives: 74.2 us -> 64.1 us
  waiting for transfers between devices: 45.7 us -> 48.9 us
    gather x2 -> x0, local copies, waits for them, and re-layouts: 18 us -> none  [shards(): jnp.take_along_axis(returned, positions, axis=1)]
    all_gather x2 -> x1, blocking collectives: 25.6 us -> 15 us  [shards(): packed_all = lax.all_gather(packed, 'ctx', axis=0, tiled=False)]
    all_to_all x1, waiting for transfers between devices: 0.01 us -> 4.62 us  [shards(): lax.all_to_all(partial_grad, 'exp', split_axis=0, concat_axis=0, tiled=True)]
    unnamed x21 -> x20, local copies, waits for them, and re-layouts: 20.7 us -> 20.7 us
  transfers between devices with their start and end apart: 3 -> 3, of which waited for: 2 -> 3; matrix products, arithmetic and copies ran while one was open for 17% -> 20% of each run, Pallas kernels for 0% -> 0%
where the time goes in v2:
time: 184 us
  blocking collectives  64.1 us (35%)
  waiting for transfers between devices  48.9 us (27%)
  local copies, waits for them, and re-layouts  33.4 us (18%)
  between operations  14.3 us (8%)
  matrix products  12.5 us (7%)
  other arithmetic  6.83 us (4%)
  starting transfers between devices  3.73 us (2%)
    all_to_all x1, blocking collectives, shards(): lax.all_to_all(send_rows, 'exp', split_axis=0, concat_axis=0, tiled=True)  32.9 us
    all_gather x1, waiting for transfers between devices, shards(): rows_all = lax.all_gather(out_grad, 'ctx', axis=0, tiled=False)  26.6 us
    unnamed x20, local copies, waits for them, and re-layouts  20.7 us
    all_gather x1, waiting for transfers between devices, shards(): hidden_all = lax.all_gather(saved_hidden[0], 'ctx', axis=0, tiled=False)  17 us
    psum x1, blocking collectives, shards(): returned = lax.psum(returned, 'ctx')  16.2 us
    all_gather x1, blocking collectives, shards(): packed_all = lax.all_gather(packed, 'ctx', axis=0, tiled=False)  15 us
    dot_general x1, matrix products, shards(): jnp.einsum('csekf,efn->scekn', hidden_all, down_weight, preferred_element...  5.48 us
    all_to_all x1, waiting for transfers between devices, shards(): lax.all_to_all(partial_grad, 'exp', split_axis=0, concat_axis=0, tiled=True)  4.62 us
  transfers between devices with their start and end apart: 3, of which 3 were waited for; matrix products, arithmetic and copies ran while one was open for 20% of the time, Pallas kernels for 0%

profile of v2, /device:TPU:0, one launch (start us, length us, event | category | flops | bytes accessed | tf_op | source)
XLA Modules:
  0.0 183.8 jit_solution(2515007388869619267)
XLA Ops:
  7.2 0.7 all-gather.7.cloned.1.call-update
  8.0 2.2 %copy.41 = bf16[1,8,2,36,768]{4,3,1,0,2:T(8,128)(2,1)} copy(bf16[1,8,2,36,768]{4,2,3,1,0:T(2,128)(2,1)} %param.10) | data formatting | bytes 1769472 | tf_op args[3]
  10.3 15.0 %all-gather.1 = f32[512,8]{0,1:T(8,128)S(1)} all-gather(f32[128,8]{0,1:T(8,128)S(1)} %pad_maximum_fusion), channel_id=3, replica_groups=mesh['ctx'=4,'exp'=8] {'ctx'}, dimensions={0}, use_global_device_ids=true | all-gather | bytes 20480 | tf_op jit(solution)/shard_map/all_gather | solution.py:26
  26.0 4.6 %reduce-window.6 = s32[4,16,4,128]{3,1,2,0:T(8,128)S(1)} reduce-window(s32[4,16,4,128]{3,1,2,0:T(8,128)S(1)} %fusion.7, s32[]{:T(128)} %constant.46.clone.1), window={size=1x1x1x128 pad=0_0x0_0x0_0x127_0}, to_apply=%region_0.0 | reduce-window | flops 4161536 | bytes 262148 | tf_op jit(solution)/shard_map/reduce-window
  31.4 26.6 %all-gather.7.cloned.1.call-done = bf16[512,2048]{1,0:T(8,128)(2,1)} async-done(((bf16[128,2048]{1,0:T(8,128)(2,1)}), bf16[512,2048]{1,0:T(8,128)(2,1)}) %all-gather.7.cloned.1.call-update) | async-done | bytes 2097168 | tf_op jit(solution)/shard_map/all_gather | solution.py:24
  58.0 1.1 constant_dynamic-slice_fusion.1
  59.1 1.9 %broadcast_in_dim.51 = bf16[4,128,4,512]{3,2,1,0:T(4,128)(2,1)} broadcast(bf16[4,128,512]{2,1,0:T(8,128)(2,1)S(1)} %constant_dynamic-slice_fusion.1), dimensions={0,1,3} | broadcast | bytes 2621440 | tf_op jit(solution)/shard_map/broadcast_in_dim | solution.py:33
  61.0 4.0 %reshape.204 = bf16[2048,512]{1,0:T(8,128)(2,1)} reshape(bf16[4,128,4,512]{3,2,1,0:T(4,128)(2,1)} %broadcast_in_dim.51) | data formatting | bytes 4194304 | tf_op jit(solution)/shard_map/reshape | solution.py:33
  65.0 11.7 %scatter_custom_fusion = bf16[2304,512]{1,0:T(8,128)(2,1)} fusion(s32[2048]{0:T(1024)S(1)} %bitcast.55, bf16[2048,512]{1,0:T(8,128)(2,1)} %reshape.204, bf16[]{:T(256)} %constant.47.clone.1), kind=kCustom, calls=%fused_computation.8 | custom fusion | bytes 2359808
  76.7 5.9 %reshape.200 = bf16[8,4,36,2,512]{4,3,2,1,0:T(2,128)(2,1)} reshape(bf16[2304,512]{1,0:T(8,128)(2,1)} %scatter_custom_fusion) | data formatting | bytes 4718592
  82.6 2.9 %copy.39 = bf16[8,4,2,36,512]{4,1,3,2,0:T(4,128)(2,1)S(1)} copy(bf16[8,4,2,36,512]{4,2,3,1,0:T(2,128)(2,1)} %bitcast.47) | data formatting | bytes 4718592 | tf_op jit(solution)/shard_map/scatter | solution.py:37
  85.5 32.9 %all_to_all.10 = bf16[8,4,2,36,512]{4,1,3,2,0:T(4,128)(2,1)} all-to-all(bf16[8,4,2,36,512]{4,1,3,2,0:T(4,128)(2,1)S(1)} %copy.39), channel_id=1, replica_groups=mesh['ctx'=4,'exp'=8] {'exp'}, dimensions={0} | all-to-all | bytes 4718592 | tf_op jit(solution)/shard_map/all_to_all | solution.py:38
  118.4 17.0 %all-gather.5.cloned.1.call-done = bf16[4,8,2,36,768]{4,3,1,0,2:T(8,128)(2,1)} async-done(((bf16[1,8,2,36,768]{4,3,1,0,2:T(8,128)(2,1)}), bf16[4,8,2,36,768]{4,3,1,0,2:T(8,128)(2,1)}) %all-gather.5.cloned.1.call-update) | async-done | bytes 3538960 | tf_op jit(solution)/shard_map/all_gather | solution.py:29
  135.4 5.5 %fusion = f32[8,4,2,36]{3,0,1,2:T(8,128)S(1)} fusion(bf16[8,4,2,36,512]{4,1,3,2,0:T(4,128)(2,1)} %all_to_all.10, bf16[4,8,2,36,768]{4,3,1,0,2:T(8,128)(2,1)} %all-gather.5.cloned.1.call-done, bf16[2,768,512]{2,1,0:T(8,128)(2,1)S(1)} %copy-done), kind=kOutput, calls=%fused_computation.2 | convolution fusion | flops 1817835264 | bytes 7480320 | tf_op jit(solution)/shard_map/csekf,efn->scekn/dot_general | solution.py:39
  140.9 0.7 reshape.216
  141.7 3.7 %all-to-all-start.1 = ((f32[8,1,288]{2,1,0:T(1,128)}), f32[8,1,288]{2,1,0:T(1,128)S(1)}, u32[]{:S(2)}, u32[]{:S(2)}) async-start(f32[8,1,288]{2,1,0:T(1,128)} %reshape.216), calls=%async_computation.1 | async-start | bytes 24576 | tf_op jit(solution)/shard_map/all_to_all | solution.py:43
  145.4 4.6 %all-to-all-done.1 = f32[8,1,288]{2,1,0:T(1,128)S(1)} async-done(((f32[8,1,288]{2,1,0:T(1,128)}), f32[8,1,288]{2,1,0:T(1,128)S(1)}, u32[]{:S(2)}, u32[]{:S(2)}) %all-to-all-start.1) | async-done | bytes 9248 | tf_op jit(solution)/shard_map/all_to_all | solution.py:43
  150.0 0.5 broadcast.206
  150.6 0.7 reduce.6
  151.5 16.2 %psum.7 = f32[4,576]{1,0:T(4,128)S(1)} all-reduce(f32[4,576]{1,0:T(4,128)S(1)} %broadcast_in_dim.52), channel_id=1, replica_groups=mesh['ctx'=4,'exp'=8] {'ctx'}, use_global_device_ids=true, to_apply=%region_5.6 | all-reduce | flops 2304 | bytes 18432 | tf_op jit(solution)/shard_map/psum | solution.py:44
  167.7 0.7 select_reduce_fusion
  169.2 0.7 copy.45
  169.9 3.7 %add_convert_fusion = bf16[4,128,2048]{2,1,0:T(8,128)(2,1)S(1)} fusion(bf16[4,128,2048]{2,1,0:T(8,128)(2,1)} %bitcast.52, f32[4,128,16]{1,2,0:T(8,128)S(1)} %select_reduce_fusion.1, bf16[2048,16]{0,1:T(8,128)(2,1)S(1)} %copy-done.1), kind=kOutput, calls=%fused_computation.5 | convolution fusion | flops 204472320 | bytes 4292608 | tf_op jit(solution)/shard_map/dot_general | solution.py:56
  173.6 3.3 %convolution_convert_fusion = bf16[512,1024]{1,0:T(8,128)(2,1)} fusion(bf16[512,2048]{1,0:T(8,128)(2,1)S(1)} %bitcast.53, bf16[1024,2048]{1,0:T(8,128)(2,1)S(1)} %copy-done.6), kind=kOutput, calls=%fused_computation.7 | convolution fusion | flops 2148007936 | bytes 7340032 | tf_op jit(solution)/shard_map/dot_general | solution.py:60
  (47 shorter events, 2.8 us)
Async XLA Ops:
  7.2 128.2 %copy-start = (bf16[2,768,512]{2,1,0:T(8,128)(2,1)S(1)}, bf16[2,768,512]{2,1,0:T(8,128)(2,1)}, u32[]{:S(2)}) copy-start(bf16[2,768,512]{2,1,0:T(8,128)(2,1)} %param.11) | copy-start | bytes 4718596
  7.2 3.1 %copy-start.2 = (s32[128,4]{0,1:T(4,128)S(1)}, s32[128,4]{0,1:T(4,128)}, u32[]{:S(2)}) copy-start(s32[128,4]{0,1:T(4,128)} %param.8) | copy-start | bytes 6148
  7.2 3.1 %copy-start.3 = (f32[128,4]{0,1:T(4,128)S(1)}, f32[128,4]{0,1:T(4,128)}, u32[]{:S(2)}) copy-start(f32[128,4]{0,1:T(4,128)} %param.9) | copy-start | bytes 6148
  7.2 50.8 %all-gather.7.cloned.1.call-start = ((), (), s32[]{:S(2)}) async-start(), calls=%async_computation.3 | async-start | bytes 2621440 | tf_op jit(solution)/shard_map/all_gather | solution.py:24
  7.9 23.3 %copy-start.5 = (s32[4]{0:T(128)S(1)}, s32[4]{0:T(128)}, u32[]{:S(2)}) copy-start(s32[4]{0:T(128)} %constant.59) | copy-start | bytes 52
  7.9 23.4 %copy-start.4 = (s32[4]{0:T(128)S(1)}, s32[4]{0:T(128)}, u32[]{:S(2)}) copy-start(s32[4]{0:T(128)} %constant.62) | copy-start | bytes 52
  8.0 127.5 %all-gather.5.cloned.1.call-start = ((), (), s32[]{:S(2)}) async-start(), calls=%async_computation.2 | async-start | bytes 4915200 | tf_op jit(solution)/shard_map/all_gather | solution.py:29
  140.9 29.0 %copy-start.1 = (bf16[2048,16]{0,1:T(8,128)(2,1)S(1)}, bf16[2048,16]{0,1:T(8,128)(2,1)}, u32[]{:S(2)}) copy-start(bf16[2048,16]{0,1:T(8,128)(2,1)} %param.12) | copy-start | bytes 196612
  141.7 8.4 %all-to-all-start.1 = ((f32[8,1,288]{2,1,0:T(1,128)}), f32[8,1,288]{2,1,0:T(1,128)S(1)}, u32[]{:S(2)}, u32[]{:S(2)}) async-start(f32[8,1,288]{2,1,0:T(1,128)} %reshape.216), calls=%async_computation.1 | async-start | bytes 24576 | tf_op jit(solution)/shard_map/all_to_all | solution.py:43
  169.9 3.7 %copy-start.6 = (bf16[1024,2048]{1,0:T(8,128)(2,1)S(1)}, bf16[1024,2048]{1,0:T(8,128)(2,1)}, u32[]{:S(2)}) copy-start(bf16[1024,2048]{1,0:T(8,128)(2,1)} %param.13) | copy-start | bytes 12582916
Sparse Core Ops, SparseCore 0:
  9.6 48.4 all-gather.6
  60.2 75.1 all-gather.4

commit v3 on v2

--- a/solution.py
+++ b/solution.py
@@ -26,7 +26,19 @@
     packed_all = lax.all_gather(packed, "ctx", axis=0, tiled=False)
     ids_all = packed_all[:, :, :top_count].astype(jnp.int32)
     probs_all = packed_all[:, :, top_count:]
-    hidden_all = lax.all_gather(saved_hidden[0], "ctx", axis=0, tiled=False)
+    own = saved_hidden[0]
+    right, left, from_left, from_right = own, own, [], []
+    for _ in range(n_ctx - 1):
+        right = lax.ppermute(right, "ctx", [(i, i + 1) for i in range(n_ctx - 1)])
+        left = lax.ppermute(left, "ctx", [(i + 1, i) for i in range(n_ctx - 1)])
+        from_left.append(right)
+        from_right.append(left)
+    hidden_all = jnp.zeros((n_ctx,) + own.shape, own.dtype)
+    for k in range(n_ctx - 1, 0, -1):
+        hidden_all = lax.dynamic_update_index_in_dim(hidden_all, from_left[k - 1], jnp.maximum(me_ctx - k, 0), 0)
+    for k in range(n_ctx - 1, 0, -1):
+        hidden_all = lax.dynamic_update_index_in_dim(hidden_all, from_right[k - 1], jnp.minimum(me_ctx + k, n_ctx - 1), 0)
+    hidden_all = lax.dynamic_update_index_in_dim(hidden_all, own, me_ctx, 0)
     flat_ids, slot_rank = jax.vmap(lambda r: route_ranks(r, experts))(ids_all)
     positions = flat_ids * capacity + slot_rank
     cols = lax.dynamic_slice_in_dim(rows_all, me_ctx * dslice, dslice, axis=2)

time: 184 us -> 221 us (1.20)
  starting transfers between devices: 3.73 us -> 39 us
  blocking collectives: 64.1 us -> 47.8 us
  local copies, waits for them, and re-layouts: 33.4 us -> 48 us
  other arithmetic: 6.83 us -> 9.51 us
    ppermute x0 -> x6, waiting for transfers between devices: none -> 43.3 us  [the longest x3 29.6 us: shards(): right = lax.ppermute(right, 'ctx', [(i, i + 1) for i in range(n_ctx - 1)])]
    all_to_all x1 -> x0, blocking collectives: 32.9 us -> none  [shards(): lax.all_to_all(send_rows, 'exp', split_axis=0, concat_axis=0, tiled=True)]
    ppermute x0 -> x6, starting transfers between devices: none -> 30.7 us  [the longest x3 26.7 us: shards(): right = lax.ppermute(right, 'ctx', [(i, i + 1) for i in range(n_ctx - 1)])]
    all_gather x1, waiting for transfers between devices: 26.6 us -> 0.02 us  [shards(): rows_all = lax.all_gather(out_grad, 'ctx', axis=0, tiled=False)]
    all_gather x1 -> x0, waiting for transfers between devices: 17 us -> none  [shards(): hidden_all = lax.all_gather(saved_hidden[0], 'ctx', axis=0, tiled=False)]
    all_gather x1, blocking collectives: 15 us -> 31.7 us  [shards(): packed_all = lax.all_gather(packed, 'ctx', axis=0, tiled=False)]
    dynamic_update_slice x0 -> x7, local copies, waits for them, and re-layouts: none -> 13.4 us  [the longest x3 6.78 us: shards(): lax.dynamic_update_index_in_dim(hidden_all, from_left[k - 1], jnp.maximum...]
    all_to_all x0 -> x1, starting transfers between devices: none -> 4.38 us  [shards(): lax.all_to_all(send_rows, 'exp', split_axis=0, concat_axis=0, tiled=True)]
  transfers between devices with their start and end apart: 3 -> 9, of which waited for: 3 -> 3; matrix products, arithmetic and copies ran while one was open for 20% -> 24% of each run, Pallas kernels for 0% -> 0%
where the time goes in v3:
time: 221 us; the launch traced here: 220 us
  waiting for transfers between devices  48.6 us (22%)
  local copies, waits for them, and re-layouts  48 us (22%)
  blocking collectives  47.8 us (22%)
  starting transfers between devices  39 us (18%)
  between operations  14.3 us (6%)
  matrix products  12.6 us (6%)
  other arithmetic  9.51 us (4%)
    all_gather x1, blocking collectives, shards(): packed_all = lax.all_gather(packed, 'ctx', axis=0, tiled=False)  31.7 us
    ppermute x3, waiting for transfers between devices, shards(): right = lax.ppermute(right, 'ctx', [(i, i + 1) for i in range(n_ctx - 1)])  29.6 us
    ppermute x3, starting transfers between devices, shards(): right = lax.ppermute(right, 'ctx', [(i, i + 1) for i in range(n_ctx - 1)])  26.7 us
    unnamed x13, local copies, waits for them, and re-layouts  18.4 us
    psum x1, blocking collectives, shards(): returned = lax.psum(returned, 'ctx')  16.1 us
    ppermute x3, waiting for transfers between devices, shards(): left = lax.ppermute(left, 'ctx', [(i + 1, i) for i in range(n_ctx - 1)])  13.7 us
    dynamic_update_slice x3, local copies, waits for them, and re-layouts, shards(): lax.dynamic_update_index_in_dim(hidden_all, from_left[k - 1], jnp.maximum...  6.78 us
    dot_general x1, matrix products, shards(): jnp.einsum('csekf,efn->scekn', hidden_all, down_weight, preferred_element...  5.59 us
  transfers between devices with their start and end apart: 9, of which 3 were waited for; matrix products, arithmetic and copies ran while one was open for 24% of the time, Pallas kernels for 0%

profile of v3, /device:TPU:0, one launch (start us, length us, event | category | flops | bytes accessed | tf_op | source)
XLA Modules:
  0.0 219.9 jit_solution(10738357573883738285)
XLA Ops:
  7.9 5.9 %collective-permute-start = (bf16[8,2,36,768]{3,1,2,0:T(2,128)(2,1)}, bf16[8,2,36,768]{3,1,2,0:T(2,128)(2,1)}, u32[]{:S(2)}, u32[]{:S(2)}) collective-permute-start(bf16[8,2,36,768]{3,1,2,0:T(2,128)(2,1)} %bitcast.61), channel_id=1, source_target_pairs={{0,8},{8,16},{16,24},{1,9},{9,17},{17,25},{2,10},{10,18},{18,26},{... | collective-permute-start | bytes 2654216 | tf_op jit(solution)/shard_map/ppermute | solution.py:32
  15.1 29.6 %collective-permute-done = bf16[8,2,36,768]{3,1,2,0:T(2,128)(2,1)} collective-permute-done((bf16[8,2,36,768]{3,1,2,0:T(2,128)(2,1)}, bf16[8,2,36,768]{3,1,2,0:T(2,128)(2,1)}, u32[]{:S(2)}, u32[]{:S(2)}) %collective-permute-start) | collective-permute-done | bytes 884768 | tf_op jit(solution)/shard_map/ppermute | solution.py:32
  44.6 15.3 %collective-permute-start.1 = (bf16[8,2,36,768]{3,1,2,0:T(2,128)(2,1)}, bf16[8,2,36,768]{3,1,2,0:T(2,128)(2,1)}, u32[]{:S(2)}, u32[]{:S(2)}) collective-permute-start(bf16[8,2,36,768]{3,1,2,0:T(2,128)(2,1)} %collective-permute-done), channel_id=1, source_target_pairs={{0,8},{8,16},{16,24},{1,9},{9,17},{17,25},{2,10},{10,18},{18,26},{... | collective-permute-start | bytes 2654216 | tf_op jit(solution)/shard_map/ppermute | solution.py:32
  61.3 31.7 %all-gather.1 = f32[512,8]{0,1:T(8,128)S(1)} all-gather(f32[128,8]{0,1:T(8,128)S(1)} %pad_maximum_fusion), channel_id=3, replica_groups=mesh['ctx'=4,'exp'=8] {'ctx'}, dimensions={0}, use_global_device_ids=true | all-gather | bytes 20480 | tf_op jit(solution)/shard_map/all_gather | solution.py:26
  93.8 4.6 %reduce-window.6 = s32[4,16,4,128]{3,1,2,0:T(8,128)S(1)} reduce-window(s32[4,16,4,128]{3,1,2,0:T(8,128)S(1)} %fusion.7, s32[]{:T(128)} %constant.71.clone.1), window={size=1x1x1x128 pad=0_0x0_0x0_0x127_0}, to_apply=%region_0.1 | reduce-window | flops 4161536 | bytes 262148 | tf_op jit(solution)/shard_map/reduce-window
  100.3 5.5 %collective-permute-start.2 = (bf16[8,2,36,768]{3,1,2,0:T(2,128)(2,1)}, bf16[8,2,36,768]{3,1,2,0:T(2,128)(2,1)}, u32[]{:S(2)}, u32[]{:S(2)}) collective-permute-start(bf16[8,2,36,768]{3,1,2,0:T(2,128)(2,1)} %collective-permute-done.1), channel_id=1, source_target_pairs={{0,8},{8,16},{16,24},{1,9},{9,17},{17,25},{2,10},{10,18},{18,26},{... | collective-permute-start | bytes 2654216 | tf_op jit(solution)/shard_map/ppermute | solution.py:32
  110.3 4.0 %reshape.204 = bf16[2048,512]{1,0:T(8,128)(2,1)} reshape(bf16[4,128,4,512]{3,2,1,0:T(4,128)(2,1)} %broadcast_in_dim.74) | data formatting | bytes 4194304 | tf_op jit(solution)/shard_map/reshape | solution.py:45
  114.3 11.6 %scatter_custom_fusion = bf16[2304,512]{1,0:T(8,128)(2,1)} fusion(s32[2048]{0:T(1024)S(1)} %bitcast.65, bf16[2048,512]{1,0:T(8,128)(2,1)} %reshape.204, bf16[]{:T(256)} %constant.72.clone.1), kind=kCustom, calls=%fused_computation.8 | custom fusion | bytes 2359808
  125.9 5.9 %reshape.200 = bf16[8,4,36,2,512]{4,3,2,1,0:T(2,128)(2,1)} reshape(bf16[2304,512]{1,0:T(8,128)(2,1)} %scatter_custom_fusion) | data formatting | bytes 4718592
  131.8 4.3 %copy.69 = bf16[8,4,2,36,512]{4,1,3,2,0:T(4,128)(2,1)} copy(bf16[8,4,2,36,512]{4,2,3,1,0:T(2,128)(2,1)} %bitcast.54) | data formatting | bytes 4718592 | tf_op jit(solution)/shard_map/scatter | solution.py:49
  136.1 4.4 %all-to-all-start = ((bf16[8,4,2,36,512]{4,1,3,2,0:T(4,128)(2,1)}), bf16[8,4,2,36,512]{4,1,3,2,0:T(4,128)(2,1)}, u32[]{:S(2)}, u32[]{:S(2)}) async-start(bf16[8,4,2,36,512]{4,1,3,2,0:T(4,128)(2,1)} %copy.69), calls=%async_computation | async-start | bytes 4718592 | tf_op jit(solution)/shard_map/all_to_all | solution.py:50
  142.0 2.1 broadcast_in_dim.75
  144.2 2.2 %copy_dynamic-update-slice_fusion.6 = bf16[4,8,2,36,768]{4,3,1,0,2:T(8,128)(2,1)} fusion(bf16[4,8,2,36,768]{4,3,1,0,2:T(8,128)(2,1)} %broadcast_in_dim.75, s32[]{:T(128)S(6)} %max.9, bf16[1,8,2,36,768]{4,2,3,1,0:T(2,128)(2,1)} %bitcast.6), kind=kLoop, calls=%fused_computation.16 | loop fusion | bytes 1867780 | tf_op jit(solution)/shard_map/jit(dynamic_update_index_in_dim)/dynamic_update_slice | solution.py:38
  146.4 2.2 %copy_dynamic-update-slice_fusion.5 = bf16[4,8,2,36,768]{4,3,1,0,2:T(8,128)(2,1)} fusion(bf16[4,8,2,36,768]{4,3,1,0,2:T(8,128)(2,1)} %copy_dynamic-update-slice_fusion.6, s32[]{:T(128)S(6)} %max.10, bf16[1,8,2,36,768]{4,2,3,1,0:T(2,128)(2,1)} %bitcast.7), kind=kLoop, calls=%fused_computation.15 | loop fusion | bytes 1867780 | tf_op jit(solution)/shard_map/jit(dynamic_update_index_in_dim)/dynamic_update_slice | solution.py:38
  148.6 2.3 %copy_dynamic-update-slice_fusion.4 = bf16[4,8,2,36,768]{4,3,1,0,2:T(8,128)(2,1)} fusion(bf16[4,8,2,36,768]{4,3,1,0,2:T(8,128)(2,1)} %copy_dynamic-update-slice_fusion.5, s32[]{:T(128)S(6)} %max.11, bf16[1,8,2,36,768]{4,2,3,1,0:T(2,128)(2,1)} %bitcast.8), kind=kLoop, calls=%fused_computation.14 | loop fusion | bytes 1867780 | tf_op jit(solution)/shard_map/jit(dynamic_update_index_in_dim)/dynamic_update_slice | solution.py:38
  151.0 13.7 %collective-permute-done.5 = bf16[8,2,36,768]{3,1,2,0:T(2,128)(2,1)} collective-permute-done((bf16[8,2,36,768]{3,1,2,0:T(2,128)(2,1)}, bf16[8,2,36,768]{3,1,2,0:T(2,128)(2,1)}, u32[]{:S(2)}, u32[]{:S(2)}) %collective-permute-start.5) | collective-permute-done | bytes 884768 | tf_op jit(solution)/shard_map/ppermute | solution.py:33
  164.7 2.2 %copy_dynamic-update-slice_fusion.3 = bf16[4,8,2,36,768]{4,3,1,0,2:T(8,128)(2,1)} fusion(bf16[4,8,2,36,768]{4,3,1,0,2:T(8,128)(2,1)} %copy_dynamic-update-slice_fusion.4, s32[]{:T(128)S(6)} %select_n.93, bf16[1,8,2,36,768]{4,2,3,1,0:T(2,128)(2,1)} %bitcast.9), kind=kLoop, calls=%fused_computation.13 | loop fusion | bytes 1867780 | tf_op jit(solution)/shard_map/jit(dynamic_update_index_in_dim)/dynamic_update_slice | solution.py:40
  166.9 2.2 %copy_dynamic-update-slice_fusion.2 = bf16[4,8,2,36,768]{4,3,1,0,2:T(8,128)(2,1)} fusion(bf16[4,8,2,36,768]{4,3,1,0,2:T(8,128)(2,1)} %copy_dynamic-update-slice_fusion.3, s32[]{:T(128)S(6)} %select_n.94, bf16[1,8,2,36,768]{4,2,3,1,0:T(2,128)(2,1)} %bitcast.10), kind=kLoop, calls=%fused_computation.12 | loop fusion | bytes 1867780 | tf_op jit(solution)/shard_map/jit(dynamic_update_index_in_dim)/dynamic_update_slice | solution.py:40
  171.3 5.6 %fusion = f32[8,4,2,36]{3,0,1,2:T(8,128)S(1)} fusion(bf16[8,4,2,36,512]{4,1,3,2,0:T(4,128)(2,1)} %all-to-all-done, bf16[4,8,2,36,768]{4,3,1,0,2:T(8,128)(2,1)} %copy_dynamic-update-slice_fusion, bf16[2,768,512]{2,1,0:T(8,128)(2,1)S(1)} %copy-done), kind=kOutput, calls=%fused_computation.2 | convolution fusion | flops 1817835264 | bytes 7480320 | tf_op jit(solution)/shard_map/csekf,efn->scekn/dot_general | solution.py:51
  177.6 3.8 %all-to-all-start.1 = ((f32[8,1,288]{2,1,0:T(1,128)}), f32[8,1,288]{2,1,0:T(1,128)S(1)}, u32[]{:S(2)}, u32[]{:S(2)}) async-start(f32[8,1,288]{2,1,0:T(1,128)} %reshape.216), calls=%async_computation.1 | async-start | bytes 24576 | tf_op jit(solution)/shard_map/all_to_all | solution.py:55
  181.6 4.6 %all-to-all-done.1 = f32[8,1,288]{2,1,0:T(1,128)S(1)} async-done(((f32[8,1,288]{2,1,0:T(1,128)}), f32[8,1,288]{2,1,0:T(1,128)S(1)}, u32[]{:S(2)}, u32[]{:S(2)}) %all-to-all-start.1) | async-done | bytes 9248 | tf_op jit(solution)/shard_map/all_to_all | solution.py:55
  187.6 16.1 %psum.7 = f32[4,576]{1,0:T(4,128)S(1)} all-reduce(f32[4,576]{1,0:T(4,128)S(1)} %broadcast_in_dim.82), channel_id=1, replica_groups=mesh['ctx'=4,'exp'=8] {'ctx'}, use_global_device_ids=true, to_apply=%region_5.6 | all-reduce | flops 2304 | bytes 18432 | tf_op jit(solution)/shard_map/psum | solution.py:56
  206.0 3.7 %add_convert_fusion = bf16[4,128,2048]{2,1,0:T(8,128)(2,1)S(1)} fusion(bf16[4,128,2048]{2,1,0:T(8,128)(2,1)} %bitcast.59, f32[4,128,16]{1,2,0:T(8,128)S(1)} %select_reduce_fusion.1, bf16[2048,16]{0,1:T(8,128)(2,1)S(1)} %copy-done.2), kind=kOutput, calls=%fused_computation.5 | convolution fusion | flops 204472320 | bytes 4292608 | tf_op jit(solution)/shard_map/dot_general | solution.py:68
  209.7 3.3 %convolution_convert_fusion = bf16[512,1024]{1,0:T(8,128)(2,1)} fusion(bf16[512,2048]{1,0:T(8,128)(2,1)S(1)} %bitcast.60, bf16[1024,2048]{1,0:T(8,128)(2,1)S(1)} %copy-done.3), kind=kOutput, calls=%fused_computation.7 | convolution fusion | flops 2148007936 | bytes 7340032 | tf_op jit(solution)/shard_map/dot_general | solution.py:72
  (58 shorter events, 18.6 us)
Async XLA Ops:
  7.2 164.1 %copy-start = (bf16[2,768,512]{2,1,0:T(8,128)(2,1)S(1)}, bf16[2,768,512]{2,1,0:T(8,128)(2,1)}, u32[]{:S(2)}) copy-start(bf16[2,768,512]{2,1,0:T(8,128)(2,1)} %param.11) | copy-start | bytes 4718596
  7.2 100.1 %all-gather.4.cloned.1.call-start = ((), (), s32[]{:S(2)}) async-start(), calls=%async_computation.2 | async-start | bytes 2621440 | tf_op jit(solution)/shard_map/all_gather | solution.py:24
  7.9 36.7 %collective-permute-start = (bf16[8,2,36,768]{3,1,2,0:T(2,128)(2,1)}, bf16[8,2,36,768]{3,1,2,0:T(2,128)(2,1)}, u32[]{:S(2)}, u32[]{:S(2)}) collective-permute-start(bf16[8,2,36,768]{3,1,2,0:T(2,128)(2,1)} %bitcast.61), channel_id=1, source_target_pairs={{0,8},{8,16},{16,24},{1,9},{9,17},{17,25},{2,10},{10,18},{18,26},{... | collective-permute-start | bytes 2654216 | tf_op jit(solution)/shard_map/ppermute | solution.py:32
  13.8 85.1 %collective-permute-start.3 = (bf16[8,2,36,768]{3,1,2,0:T(2,128)(2,1)}, bf16[8,2,36,768]{3,1,2,0:T(2,128)(2,1)S(1)}, u32[]{:S(2)}, u32[]{:S(2)}) collective-permute-start(bf16[8,2,36,768]{3,1,2,0:T(2,128)(2,1)} %bitcast.62), channel_id=1, source_target_pairs={{8,0},{16,8},{24,16},{9,1},{17,9},{25,17},{10,2},{18,10},{26,18},{... | collective-permute-start | bytes 2654216 | tf_op jit(solution)/shard_map/ppermute | solution.py:33
  44.6 55.6 %collective-permute-start.1 = (bf16[8,2,36,768]{3,1,2,0:T(2,128)(2,1)}, bf16[8,2,36,768]{3,1,2,0:T(2,128)(2,1)}, u32[]{:S(2)}, u32[]{:S(2)}) collective-permute-start(bf16[8,2,36,768]{3,1,2,0:T(2,128)(2,1)} %collective-permute-done), channel_id=1, source_target_pairs={{0,8},{8,16},{16,24},{1,9},{9,17},{17,25},{2,10},{10,18},{18,26},{... | collective-permute-start | bytes 2654216 | tf_op jit(solution)/shard_map/ppermute | solution.py:32
  99.0 41.6 %collective-permute-start.4 = (bf16[8,2,36,768]{3,1,2,0:T(2,128)(2,1)S(1)}, bf16[8,2,36,768]{3,1,2,0:T(2,128)(2,1)}, u32[]{:S(2)}, u32[]{:S(2)}) collective-permute-start(bf16[8,2,36,768]{3,1,2,0:T(2,128)(2,1)S(1)} %collective-permute-done.3), channel_id=1, source_target_pairs={{8,0},{16,8},{24,16},{9,1},{17,9},{25,17},{10,2},{18,10},{26,18},{... | collective-permute-start | bytes 2654216 | tf_op jit(solution)/shard_map/ppermute | solution.py:33
  100.3 41.8 %collective-permute-start.2 = (bf16[8,2,36,768]{3,1,2,0:T(2,128)(2,1)}, bf16[8,2,36,768]{3,1,2,0:T(2,128)(2,1)}, u32[]{:S(2)}, u32[]{:S(2)}) collective-permute-start(bf16[8,2,36,768]{3,1,2,0:T(2,128)(2,1)} %collective-permute-done.1), channel_id=1, source_target_pairs={{0,8},{8,16},{16,24},{1,9},{9,17},{17,25},{2,10},{10,18},{18,26},{... | collective-permute-start | bytes 2654216 | tf_op jit(solution)/shard_map/ppermute | solution.py:32
  136.1 35.1 %all-to-all-start = ((bf16[8,4,2,36,512]{4,1,3,2,0:T(4,128)(2,1)}), bf16[8,4,2,36,512]{4,1,3,2,0:T(4,128)(2,1)}, u32[]{:S(2)}, u32[]{:S(2)}) async-start(bf16[8,4,2,36,512]{4,1,3,2,0:T(4,128)(2,1)} %copy.69), calls=%async_computation | async-start | bytes 4718592 | tf_op jit(solution)/shard_map/all_to_all | solution.py:50
  140.5 24.1 %collective-permute-start.5 = (bf16[8,2,36,768]{3,1,2,0:T(2,128)(2,1)}, bf16[8,2,36,768]{3,1,2,0:T(2,128)(2,1)}, u32[]{:S(2)}, u32[]{:S(2)}) collective-permute-start(bf16[8,2,36,768]{3,1,2,0:T(2,128)(2,1)} %collective-permute-done.4), channel_id=1, source_target_pairs={{8,0},{16,8},{24,16},{9,1},{17,9},{25,17},{10,2},{18,10},{26,18},{... | collective-permute-start | bytes 2654216 | tf_op jit(solution)/shard_map/ppermute | solution.py:33
  148.6 21.5 %copy-start.1 = (bf16[1,8,2,36,768]{4,2,3,1,0:T(2,128)(2,1)S(1)}, bf16[1,8,2,36,768]{4,2,3,1,0:T(2,128)(2,1)}, u32[]{:S(2)}) copy-start(bf16[1,8,2,36,768]{4,2,3,1,0:T(2,128)(2,1)} %param.10) | copy-start | bytes 2654212
  171.2 34.7 %copy-start.2 = (bf16[2048,16]{0,1:T(8,128)(2,1)S(1)}, bf16[2048,16]{0,1:T(8,128)(2,1)}, u32[]{:S(2)}) copy-start(bf16[2048,16]{0,1:T(8,128)(2,1)} %param.12) | copy-start | bytes 196612
  177.6 8.6 %all-to-all-start.1 = ((f32[8,1,288]{2,1,0:T(1,128)}), f32[8,1,288]{2,1,0:T(1,128)S(1)}, u32[]{:S(2)}, u32[]{:S(2)}) async-start(f32[8,1,288]{2,1,0:T(1,128)} %reshape.216), calls=%async_computation.1 | async-start | bytes 24576 | tf_op jit(solution)/shard_map/all_to_all | solution.py:55
  206.0 3.7 %copy-start.3 = (bf16[1024,2048]{1,0:T(8,128)(2,1)S(1)}, bf16[1024,2048]{1,0:T(8,128)(2,1)}, u32[]{:S(2)}) copy-start(bf16[1024,2048]{1,0:T(8,128)(2,1)} %param.13) | copy-start | bytes 12582916
Sparse Core Ops, SparseCore 0:
  9.6 66.6 all-gather.3

commit v4 on v2

--- a/solution.py
+++ b/solution.py
@@ -41,7 +41,7 @@
     ).astype(jnp.bfloat16)
     partial_grad = jnp.sum(arrived.astype(jnp.float32) * outputs.astype(jnp.float32), axis=4)
     returned = lax.all_to_all(partial_grad, "exp", split_axis=0, concat_axis=0, tiled=True)
-    returned = lax.psum(returned, "ctx")
+    returned = jnp.sum(lax.all_gather(returned, "ctx", axis=0, tiled=False), axis=0)
     returned = jnp.transpose(returned, (1, 0, 2, 3)).reshape(n_ctx, experts * capacity)
     picks = positions[:, :, None] == jnp.arange(experts * capacity, dtype=jnp.int32)[None, None, :]
     gate_grad = jnp.sum(jnp.where(picks, returned[:, None, :], 0.0), axis=2)

time: 184 us -> 182 us (0.989)
  blocking collectives: 64.1 us -> 61.5 us
    psum x1 -> x0, blocking collectives: 16.2 us -> none  [shards(): returned = lax.psum(returned, 'ctx')]
    all_gather x0 -> x1, blocking collectives: none -> 13.6 us  [shards(): lax.all_gather(returned, 'ctx', axis=0, tiled=False)]
where the time goes in v4:
time: 182 us; the launch traced here: 181 us
  blocking collectives  61.5 us (34%)
  waiting for transfers between devices  48.9 us (27%)
  local copies, waits for them, and re-layouts  33.4 us (18%)
  between operations  14.3 us (8%)
  matrix products  12.5 us (7%)
  other arithmetic  6.88 us (4%)
  starting transfers between devices  3.73 us (2%)
    all_to_all x1, blocking collectives, shards(): lax.all_to_all(send_rows, 'exp', split_axis=0, concat_axis=0, tiled=True)  32.9 us
    all_gather x1, waiting for transfers between devices, shards(): rows_all = lax.all_gather(out_grad, 'ctx', axis=0, tiled=False)  26.6 us
    unnamed x20, local copies, waits for them, and re-layouts  20.7 us
    all_gather x1, waiting for transfers between devices, shards(): hidden_all = lax.all_gather(saved_hidden[0], 'ctx', axis=0, tiled=False)  17 us
    all_gather x1, blocking collectives, shards(): packed_all = lax.all_gather(packed, 'ctx', axis=0, tiled=False)  15 us
    all_gather x1, blocking collectives, shards(): lax.all_gather(returned, 'ctx', axis=0, tiled=False)  13.6 us
    dot_general x1, matrix products, shards(): jnp.einsum('csekf,efn->scekn', hidden_all, down_weight, preferred_element...  5.48 us
    all_to_all x1, waiting for transfers between devices, shards(): lax.all_to_all(partial_grad, 'exp', split_axis=0, concat_axis=0, tiled=True)  4.62 us
  transfers between devices with their start and end apart: 3, of which 3 were waited for; matrix products, arithmetic and copies ran while one was open for 20% of the time, Pallas kernels for 0%

profile of v4, /device:TPU:0, one launch (start us, length us, event | category | flops | bytes accessed | tf_op | source)
XLA Modules:
  0.0 181.2 jit_solution(7866327408563910583)
XLA Ops:
  7.2 0.7 all-gather.8.cloned.1.call-update
  8.0 2.2 %copy.48 = bf16[1,8,2,36,768]{4,3,1,0,2:T(8,128)(2,1)} copy(bf16[1,8,2,36,768]{4,2,3,1,0:T(2,128)(2,1)} %param.10) | data formatting | bytes 1769472 | tf_op args[3]
  10.3 15.0 %all-gather.1 = f32[512,8]{0,1:T(8,128)S(1)} all-gather(f32[128,8]{0,1:T(8,128)S(1)} %pad_maximum_fusion), channel_id=3, replica_groups=mesh['ctx'=4,'exp'=8] {'ctx'}, dimensions={0}, use_global_device_ids=true | all-gather | bytes 20480 | tf_op jit(solution)/shard_map/all_gather | solution.py:26
  26.0 4.6 %reduce-window.6 = s32[4,16,4,128]{3,1,2,0:T(8,128)S(1)} reduce-window(s32[4,16,4,128]{3,1,2,0:T(8,128)S(1)} %fusion.7, s32[]{:T(128)} %constant.46.clone.1), window={size=1x1x1x128 pad=0_0x0_0x0_0x127_0}, to_apply=%region_0.0 | reduce-window | flops 4161536 | bytes 262148 | tf_op jit(solution)/shard_map/reduce-window
  31.4 26.6 %all-gather.8.cloned.1.call-done = bf16[512,2048]{1,0:T(8,128)(2,1)} async-done(((bf16[128,2048]{1,0:T(8,128)(2,1)}), bf16[512,2048]{1,0:T(8,128)(2,1)}) %all-gather.8.cloned.1.call-update) | async-done | bytes 2097168 | tf_op jit(solution)/shard_map/all_gather | solution.py:24
  58.0 1.1 constant_dynamic-slice_fusion.1
  59.1 1.9 %broadcast_in_dim.51 = bf16[4,128,4,512]{3,2,1,0:T(4,128)(2,1)} broadcast(bf16[4,128,512]{2,1,0:T(8,128)(2,1)S(1)} %constant_dynamic-slice_fusion.1), dimensions={0,1,3} | broadcast | bytes 2621440 | tf_op jit(solution)/shard_map/broadcast_in_dim | solution.py:33
  61.0 4.0 %reshape.204 = bf16[2048,512]{1,0:T(8,128)(2,1)} reshape(bf16[4,128,4,512]{3,2,1,0:T(4,128)(2,1)} %broadcast_in_dim.51) | data formatting | bytes 4194304 | tf_op jit(solution)/shard_map/reshape | solution.py:33
  65.0 11.7 %scatter_custom_fusion = bf16[2304,512]{1,0:T(8,128)(2,1)} fusion(s32[2048]{0:T(1024)S(1)} %bitcast.63, bf16[2048,512]{1,0:T(8,128)(2,1)} %reshape.204, bf16[]{:T(256)} %constant.47.clone.1), kind=kCustom, calls=%fused_computation.8 | custom fusion | bytes 2359808
  76.7 5.9 %reshape.200 = bf16[8,4,36,2,512]{4,3,2,1,0:T(2,128)(2,1)} reshape(bf16[2304,512]{1,0:T(8,128)(2,1)} %scatter_custom_fusion) | data formatting | bytes 4718592
  82.6 2.9 %copy.46 = bf16[8,4,2,36,512]{4,1,3,2,0:T(4,128)(2,1)S(1)} copy(bf16[8,4,2,36,512]{4,2,3,1,0:T(2,128)(2,1)} %bitcast.52) | data formatting | bytes 4718592 | tf_op jit(solution)/shard_map/scatter | solution.py:37
  85.5 32.9 %all_to_all.10 = bf16[8,4,2,36,512]{4,1,3,2,0:T(4,128)(2,1)} all-to-all(bf16[8,4,2,36,512]{4,1,3,2,0:T(4,128)(2,1)S(1)} %copy.46), channel_id=1, replica_groups=mesh['ctx'=4,'exp'=8] {'exp'}, dimensions={0} | all-to-all | bytes 4718592 | tf_op jit(solution)/shard_map/all_to_all | solution.py:38
  118.4 17.0 %all-gather.6.cloned.1.call-done = bf16[4,8,2,36,768]{4,3,1,0,2:T(8,128)(2,1)} async-done(((bf16[1,8,2,36,768]{4,3,1,0,2:T(8,128)(2,1)}), bf16[4,8,2,36,768]{4,3,1,0,2:T(8,128)(2,1)}) %all-gather.6.cloned.1.call-update) | async-done | bytes 3538960 | tf_op jit(solution)/shard_map/all_gather | solution.py:29
  135.4 5.5 %fusion = f32[8,4,2,36]{3,0,1,2:T(8,128)S(1)} fusion(bf16[8,4,2,36,512]{4,1,3,2,0:T(4,128)(2,1)} %all_to_all.10, bf16[4,8,2,36,768]{4,3,1,0,2:T(8,128)(2,1)} %all-gather.6.cloned.1.call-done, bf16[2,768,512]{2,1,0:T(8,128)(2,1)S(1)} %copy-done), kind=kOutput, calls=%fused_computation.2 | convolution fusion | flops 1817835264 | bytes 7480320 | tf_op jit(solution)/shard_map/csekf,efn->scekn/dot_general | solution.py:39
  140.9 0.7 reshape.217
  141.6 3.7 %all-to-all-start.1 = ((f32[8,1,288]{2,1,0:T(1,128)}), f32[8,1,288]{2,1,0:T(1,128)S(1)}, u32[]{:S(2)}, u32[]{:S(2)}) async-start(f32[8,1,288]{2,1,0:T(1,128)} %reshape.217), calls=%async_computation.1 | async-start | bytes 24576 | tf_op jit(solution)/shard_map/all_to_all | solution.py:43
  145.4 4.6 %all-to-all-done.1 = f32[8,1,288]{2,1,0:T(1,128)S(1)} async-done(((f32[8,1,288]{2,1,0:T(1,128)}), f32[8,1,288]{2,1,0:T(1,128)S(1)}, u32[]{:S(2)}, u32[]{:S(2)}) %all-to-all-start.1) | async-done | bytes 9248 | tf_op jit(solution)/shard_map/all_to_all | solution.py:43
  150.0 0.5 broadcast.206
  150.5 0.7 reduce.6
  151.3 13.6 %all-gather.2 = f32[32,4,2,36]{3,1,2,0:T(4,128)S(1)} all-gather(f32[8,4,2,36]{3,1,2,0:T(4,128)S(1)} %bitcast.61), channel_id=4, replica_groups=mesh['ctx'=4,'exp'=8] {'ctx'}, dimensions={0}, use_global_device_ids=true | all-gather | bytes 46080 | tf_op jit(solution)/shard_map/all_gather | solution.py:44
  165.0 0.7 select_reduce_fusion
  166.6 0.7 copy.52
  167.3 3.7 %add_convert_fusion = bf16[4,128,2048]{2,1,0:T(8,128)(2,1)S(1)} fusion(bf16[4,128,2048]{2,1,0:T(8,128)(2,1)} %bitcast.57, f32[4,128,16]{1,2,0:T(8,128)S(1)} %select_reduce_fusion.1, bf16[2048,16]{0,1:T(8,128)(2,1)S(1)} %copy-done.1), kind=kOutput, calls=%fused_computation.5 | convolution fusion | flops 204472320 | bytes 4292608 | tf_op jit(solution)/shard_map/dot_general | solution.py:56
  171.0 3.3 %convolution_convert_fusion = bf16[512,1024]{1,0:T(8,128)(2,1)} fusion(bf16[512,2048]{1,0:T(8,128)(2,1)S(1)} %bitcast.58, bf16[1024,2048]{1,0:T(8,128)(2,1)S(1)} %copy-done.6), kind=kOutput, calls=%fused_computation.7 | convolution fusion | flops 2148007936 | bytes 7340032 | tf_op jit(solution)/shard_map/dot_general | solution.py:60
  (48 shorter events, 2.9 us)
Async XLA Ops:
  7.2 128.2 %copy-start = (bf16[2,768,512]{2,1,0:T(8,128)(2,1)S(1)}, bf16[2,768,512]{2,1,0:T(8,128)(2,1)}, u32[]{:S(2)}) copy-start(bf16[2,768,512]{2,1,0:T(8,128)(2,1)} %param.11) | copy-start | bytes 4718596
  7.2 3.1 %copy-start.2 = (s32[128,4]{0,1:T(4,128)S(1)}, s32[128,4]{0,1:T(4,128)}, u32[]{:S(2)}) copy-start(s32[128,4]{0,1:T(4,128)} %param.8) | copy-start | bytes 6148
  7.2 3.1 %copy-start.3 = (f32[128,4]{0,1:T(4,128)S(1)}, f32[128,4]{0,1:T(4,128)}, u32[]{:S(2)}) copy-start(f32[128,4]{0,1:T(4,128)} %param.9) | copy-start | bytes 6148
  7.2 50.8 %all-gather.8.cloned.1.call-start = ((), (), s32[]{:S(2)}) async-start(), calls=%async_computation.3 | async-start | bytes 2621440 | tf_op jit(solution)/shard_map/all_gather | solution.py:24
  7.9 23.3 %copy-start.5 = (s32[4]{0:T(128)S(1)}, s32[4]{0:T(128)}, u32[]{:S(2)}) copy-start(s32[4]{0:T(128)} %constant.59) | copy-start | bytes 52
  7.9 23.4 %copy-start.4 = (s32[4]{0:T(128)S(1)}, s32[4]{0:T(128)}, u32[]{:S(2)}) copy-start(s32[4]{0:T(128)} %constant.62) | copy-start | bytes 52
  8.0 127.5 %all-gather.6.cloned.1.call-start = ((), (), s32[]{:S(2)}) async-start(), calls=%async_computation.2 | async-start | bytes 4915200 | tf_op jit(solution)/shard_map/all_gather | solution.py:29
  140.9 26.4 %copy-start.1 = (bf16[2048,16]{0,1:T(8,128)(2,1)S(1)}, bf16[2048,16]{0,1:T(8,128)(2,1)}, u32[]{:S(2)}) copy-start(bf16[2048,16]{0,1:T(8,128)(2,1)} %param.12) | copy-start | bytes 196612
  141.6 8.4 %all-to-all-start.1 = ((f32[8,1,288]{2,1,0:T(1,128)}), f32[8,1,288]{2,1,0:T(1,128)S(1)}, u32[]{:S(2)}, u32[]{:S(2)}) async-start(f32[8,1,288]{2,1,0:T(1,128)} %reshape.217), calls=%async_computation.1 | async-start | bytes 24576 | tf_op jit(solution)/shard_map/all_to_all | solution.py:43
  167.3 3.7 %copy-start.6 = (bf16[1024,2048]{1,0:T(8,128)(2,1)S(1)}, bf16[1024,2048]{1,0:T(8,128)(2,1)}, u32[]{:S(2)}) copy-start(bf16[1024,2048]{1,0:T(8,128)(2,1)} %param.13) | copy-start | bytes 12582916
Sparse Core Ops, SparseCore 0:
  9.6 48.4 all-gather.7
  60.2 75.1 all-gather.5
